TPU v7x, 512 devices: a whole 4x8x8 slice. The times are simulated.
512 devices in a mesh: blk: 128 (over z, y, x_lo), rep: 4 (over x_hi, core).
Axes of the slice: x: 4 (x_hi: 2, x_lo: 2; x = x_hi * 2 + x_lo), y: 8, z: 8, core: 2. Of those that a mesh axis runs over, the one named last changes fastest.
Arguments:
- left_emb: float32 [32768, 256], P('blk'), may hold values from -6 to 6
- left_state: float32 [32768], P('blk'), may hold values from 0.3 to 30
- right_emb: float32 [32768, 256], P('blk'), may hold values from -8 to 8
- right_state: float32 [32768], P('blk'), may hold values from 0.3 to 30
- relation: float32 [2, 256, 256], replicated, may hold values from -0.375 to 0.375
- relation_state: float32 [2, 256, 256], replicated, may hold values from 5242.88 to 524288
- edge_src: int32 [128, 4, 2, 2, 512], P('blk', 'rep'), may hold values from 0 to 255
- edge_dst: int32 [128, 4, 2, 2, 512], P('blk', 'rep'), may hold values from 0 to 255
- edge_rel: int32 [128, 4, 2, 2, 512], P('blk', 'rep'), may hold values from 0 to 1
- negatives: int32 [128, 4, 2, 2, 512], P('blk', 'rep'), may hold values from 0 to 255
- batch_counts: int32 [128, 4, 2], P('blk', 'rep'), may hold values from 0 to 2, as said below
Outputs:
- left_new: float32 [32768, 256], P('blk')
- left_state_new: float32 [32768], P('blk')
- right_new: float32 [32768, 256], P('blk')
- right_state_new: float32 [32768], P('blk')
- relation_new: float32 [2, 256, 256], replicated
- relation_state_new: float32 [2, 256, 256], replicated
Inputs may be any that keep to these rules, and one draw needn't show every extreme that they name: `batch_counts`: in each bucket the live edge batches of the 4 devices of one blk index number at most 4; in every draw some bucket has exactly that many, with some device at 2.
All inputs are finite; a program needn't handle non-finite values.
Results may differ from a plain program's by a relative error of at most 0.035.
Values sent between devices are 32-bit elements; how exact they have to be, the bound alone decides.
No kernel may reach another device: no remote copies, remote signals or barrier semaphores. Data moves between devices by JAX's collectives and lax.ppermute only.
A program may use at most 64 MiB of HBM per device.

v0:
```python
import jax
import jax.numpy as jnp
from jax import lax
from jax.sharding import PartitionSpec as P

learn_rate = 0.1


def from_behind(block, axis, distance):
    devices = range(lax.axis_size(axis))
    route = [((i - distance) % len(devices), i) for i in devices]
    return lax.ppermute(block, axis, route)


def batch_terms(query_table, right_bf, src_row, dst_row, rel_row, neg_row, live_flag):
    queries = query_table[rel_row, src_row]
    pos_rows = right_bf[dst_row]
    neg_rows = right_bf[neg_row]
    pos_score = jnp.sum(queries.astype(jnp.float32) * pos_rows.astype(jnp.float32), axis=-1)
    neg_score = lax.dot_general(
        queries, neg_rows, (((1,), (1,)), ((), ())), preferred_element_type=jnp.float32
    )
    row_top = jnp.maximum(jnp.max(neg_score, axis=1), pos_score)
    pos_exp = jnp.exp(pos_score - row_top)
    neg_exp = jnp.exp(neg_score - row_top[:, None])
    row_total = pos_exp + jnp.sum(neg_exp, axis=1)
    pos_weight = (pos_exp / row_total - 1.0) * live_flag
    weights = (neg_exp / row_total[:, None] * live_flag).astype(jnp.bfloat16)
    query_grad = jnp.dot(weights, neg_rows, preferred_element_type=jnp.float32) + pos_weight[
        :, None
    ] * pos_rows.astype(jnp.float32)
    neg_grad = lax.dot_general(
        weights, queries, (((0,), (0,)), ((), ())), preferred_element_type=jnp.float32
    )
    pos_grad = pos_weight[:, None] * queries.astype(jnp.float32)
    return (query_grad, neg_grad, pos_grad)


def bucket_terms(left_rows, right_rows, operator_bf, sources, targets, relations, negs, live_flags):
    left_bf = left_rows.astype(jnp.bfloat16)
    right_bf = right_rows.astype(jnp.bfloat16)
    query_table = jnp.einsum(
        "nd,rkd->rnk", left_bf, operator_bf, preferred_element_type=jnp.float32
    ).astype(jnp.bfloat16)
    nrel, rows, width = query_table.shape

    def step(position, carry):
        table_grad, right_grad = carry
        src_row = lax.dynamic_index_in_dim(sources, position, 0, keepdims=False)
        dst_row = lax.dynamic_index_in_dim(targets, position, 0, keepdims=False)
        rel_row = lax.dynamic_index_in_dim(relations, position, 0, keepdims=False)
        neg_row = lax.dynamic_index_in_dim(negs, position, 0, keepdims=False)
        live_flag = lax.dynamic_index_in_dim(live_flags, position, 0, keepdims=False)
        query_grad, neg_grad, pos_grad = batch_terms(
            query_table, right_bf, src_row, dst_row, rel_row, neg_row, live_flag
        )
        table_grad = table_grad.at[rel_row, src_row].add(query_grad)
        right_grad = right_grad.at[neg_row].add(neg_grad).at[dst_row].add(pos_grad)
        return (table_grad, right_grad)

    start = (jnp.zeros((nrel, rows, width), jnp.float32), jnp.zeros((rows, width), jnp.float32))
    table_grad, right_grad = lax.fori_loop(0, sources.shape[0], step, start)
    table_bf = table_grad.astype(jnp.bfloat16)
    left_grad = jnp.einsum("rnk,rkd->nd", table_bf, operator_bf, preferred_element_type=jnp.float32)
    operator_grad = jnp.einsum("rnk,nd->rkd", table_bf, left_bf, preferred_element_type=jnp.float32)
    return (left_grad, right_grad, operator_grad)


def row_update(embedding, accum, gradient):
    accum_next = accum + jnp.mean(gradient * gradient, axis=-1)
    return (embedding - learn_rate * gradient / jnp.sqrt(accum_next)[:, None], accum_next)


def body(
    left_emb,
    left_state,
    right_emb,
    right_state,
    relation,
    relation_state,
    edge_src,
    edge_dst,
    edge_rel,
    negatives,
    batch_counts,
):
    operator_bf = relation.astype(jnp.bfloat16)
    nbatch = edge_src.shape[3]
    left_rows, left_accum = (left_emb, left_state)
    right_rows, right_accum = (right_emb, right_state)
    operator_total = jnp.zeros(relation.shape, jnp.float32)
    for bucket in range(2):
        sources = edge_src[0, 0, bucket]
        targets = edge_dst[0, 0, bucket]
        relations = edge_rel[0, 0, bucket]
        negs = negatives[0, 0, bucket]
        live_flags = (jnp.arange(nbatch) < batch_counts[0, 0, bucket]).astype(jnp.float32)
        left_grad, right_grad, operator_grad = bucket_terms(
            left_rows, right_rows, operator_bf, sources, targets, relations, negs, live_flags
        )
        operator_total = operator_total + lax.psum(operator_grad, ("blk", "rep"))
        left_sum, right_sum = lax.psum((left_grad, right_grad), "rep")
        left_rows, left_accum = row_update(left_rows, left_accum, left_sum)
        right_rows, right_accum = row_update(right_rows, right_accum, right_sum)
        if bucket == 0:
            left_rows, left_accum = from_behind((left_rows, left_accum), "blk", 1)
    relation_state_new = relation_state + operator_total * operator_total
    relation_new = relation - learn_rate * operator_total / jnp.sqrt(relation_state_new)
    return (left_rows, left_accum, right_rows, right_accum, relation_new, relation_state_new)


def solution(mesh):
    in_specs = (
        P("blk", None),
        P("blk"),
        P("blk", None),
        P("blk"),
        P(),
        P(),
        P("blk", "rep", None, None, None),
        P("blk", "rep", None, None, None),
        P("blk", "rep", None, None, None),
        P("blk", "rep", None, None, None),
        P("blk", "rep", None),
    )
    out_specs = (P("blk", None), P("blk"), P("blk", None), P("blk"), P(), P())
    return jax.shard_map(body, mesh=mesh, in_specs=in_specs, out_specs=out_specs, check_vma=False)
```

profile of v0, /device:TPU:1, one launch (start us, length us, event | category | flops | bytes accessed | tf_op | source)
XLA Modules:
  0.0 608.4 jit_solution(12801148130178979247)
XLA Ops:
  14.1 91.3 %while.34 = (s32[]{:T(128)}, f32[2,256,256]{2,1,0:T(8,128)S(1)}, f32[256,256]{1,0:T(8,128)S(1)}, s32[2,512]{1,0:T(2,128)}, s32[2,512]{1,0:T(2,128)}, /*index=5*/...) while((s32[]{:T(128)}, f32[2,256,256]{2,1,0:T(8,128)S(1)}, ...), condition=%wide.region_7.8_spmd, body=%wide.region_0.7_spmd.sunk | while | flops 406075392 | bytes 12953801 | solution.py:62
  16.8 2.0 gather_fusion.1
  18.7 2.0 gather_fusion.2
  20.7 3.2 gather_fusion
  26.3 26.1 %scatter_fusion = f32[2,256,256]{2,1,0:T(8,128)S(1)} fusion(f32[2,256,256]{2,1,0:T(8,128)S(1)} %get-tuple-element.764, s32[512]{0:T(512)S(1)} %bitcast.154, f32[512,256]{1,0:T(8,128)S(1)} %convolution_add_fusion.5), kind=kCustom, calls=%fused_computation.6.clone.1 | custom fusion | flops 131072 | bytes 1576960 | tf_op jit(solution)/shard_map/while/body/eval_jaxpr/scatter-add | solution.py:57
  52.7 3.4 scatter_fusion.1
  56.1 3.6 scatter_custom_fusion.19
  62.4 2.0 gather_fusion.1
  64.4 2.0 gather_fusion.2
  66.3 3.2 gather_fusion
  71.9 26.1 %scatter_fusion = f32[2,256,256]{2,1,0:T(8,128)S(1)} fusion(f32[2,256,256]{2,1,0:T(8,128)S(1)} %get-tuple-element.764, s32[512]{0:T(512)S(1)} %bitcast.154, f32[512,256]{1,0:T(8,128)S(1)} %convolution_add_fusion.5), kind=kCustom, calls=%fused_computation.6.clone.1 | custom fusion | flops 131072 | bytes 1576960 | tf_op jit(solution)/shard_map/while/body/eval_jaxpr/scatter-add | solution.py:57
  98.3 3.4 scatter_fusion.1
  101.8 3.6 scatter_custom_fusion.19
  108.1 57.2 %all-reduce.10.cloned.1.call-done = (f32[256,256]{1,0:T(8,128)}, f32[256,256]{1,0:T(8,128)}) async-done(((f32[256,256]{1,0:T(8,128)}, f32[256,256]{1,0:T(8,128)}), (f32[256,256]{1,0:T(8,128)}, f32[256,256]{1,0:T(8,128)})) %all-reduce.10.cloned.1.call-update) | async-done | bytes 524304 | tf_op jit(solution)/shard_map/psum | solution.py:102
  167.8 2.5 collective-permute-start
  170.9 11.4 %collective-permute-done = f32[256,256]{1,0:T(8,128)S(1)} collective-permute-done((f32[256,256]{1,0:T(8,128)S(1)}, f32[256,256]{1,0:T(8,128)S(1)}, u32[]{:S(2)}, u32[]{:S(2)}) %collective-permute-start) | collective-permute-done | bytes 262176 | tf_op jit(solution)/shard_map/ppermute | solution.py:12
  182.7 91.3 %while.35 = (s32[]{:T(128)}, f32[2,256,256]{2,1,0:T(8,128)S(1)}, f32[256,256]{1,0:T(8,128)S(1)}, s32[2,512]{1,0:T(2,128)}, s32[2,512]{1,0:T(2,128)}, /*index=5*/...) while((s32[]{:T(128)}, f32[2,256,256]{2,1,0:T(8,128)S(1)}, ...), condition=%wide.region_19.20_spmd, body=%wide.region_12.19_spmd.sunk | while | flops 406075392 | bytes 12921097 | solution.py:62
  185.3 2.0 gather_fusion.4
  187.2 2.0 gather_fusion.5
  189.2 3.2 gather_fusion.3
  194.9 26.1 %scatter_fusion.2 = f32[2,256,256]{2,1,0:T(8,128)S(1)} fusion(f32[2,256,256]{2,1,0:T(8,128)S(1)} %get-tuple-element.797, s32[512]{0:T(512)S(1)} %bitcast.155, f32[512,256]{1,0:T(8,128)S(1)} %convolution_add_fusion.6), kind=kCustom, calls=%fused_computation.9.clone.1 | custom fusion | flops 131072 | bytes 1576960 | tf_op jit(solution)/shard_map/while/body/eval_jaxpr/scatter-add | solution.py:57
  221.3 3.4 scatter_fusion.3
  224.8 3.6 scatter_custom_fusion.23
  230.9 2.0 gather_fusion.4
  234.8 3.2 gather_fusion.3
  240.6 26.1 %scatter_fusion.2 = f32[2,256,256]{2,1,0:T(8,128)S(1)} fusion(f32[2,256,256]{2,1,0:T(8,128)S(1)} %get-tuple-element.797, s32[512]{0:T(512)S(1)} %bitcast.155, f32[512,256]{1,0:T(8,128)S(1)} %convolution_add_fusion.6), kind=kCustom, calls=%fused_computation.9.clone.1 | custom fusion | flops 131072 | bytes 1576960 | tf_op jit(solution)/shard_map/while/body/eval_jaxpr/scatter-add | solution.py:57
  267.0 3.4 scatter_fusion.3
  270.5 3.6 scatter_custom_fusion.23
  274.1 2.2 convolution_add_fusion.2
  280.0 262.9 %all-reduce.6.cloned.1.call-done = f32[2,256,256]{2,1,0:T(8,128)} async-done(((f32[2,256,256]{2,1,0:T(8,128)}), f32[2,256,256]{2,1,0:T(8,128)}) %all-reduce.6.cloned.1.call-update) | async-done | bytes 524304 | tf_op jit(solution)/shard_map/psum | solution.py:101
  542.9 2.2 multiply_subtract_fusion
  545.0 51.2 %all-reduce.8.cloned.1.call-done = (f32[256,256]{1,0:T(8,128)}, f32[256,256]{1,0:T(8,128)}) async-done(((f32[256,256]{1,0:T(8,128)}, f32[256,256]{1,0:T(8,128)}), (f32[256,256]{1,0:T(8,128)}, f32[256,256]{1,0:T(8,128)})) %all-reduce.8.cloned.1.call-update) | async-done | bytes 524304 | tf_op jit(solution)/shard_map/psum | solution.py:102
  (154 shorter events, 45.4 us)
Async XLA Ops:
  7.2 158.1 %all-reduce.10.cloned.1.call-start = ((), (), s32[]{:S(2)}) async-start(), calls=%async_computation.2 | async-start | bytes 1048576 | tf_op jit(solution)/shard_map/psum | solution.py:102
  10.6 1.1 copy-start.2
  12.0 0.7 copy-start.17
  12.0 0.7 copy-start.18
  12.7 0.7 copy-start.19
  12.7 0.7 copy-start.20
  14.1 1.2 copy-start.11
  56.1 3.6 copy-start.12
  59.7 1.2 copy-start.11
  101.8 3.6 copy-start.12
  105.4 0.9 copy-start.1
  106.3 436.5 %all-reduce.6.cloned.1.call-start = ((), (), s32[]{:S(2)}) async-start(), calls=%async_computation | async-start | bytes 1048576 | tf_op jit(solution)/shard_map/psum | solution.py:101
  165.3 1.1 copy-start.9
  166.4 3.9 copy-start.13
  166.4 0.7 copy-start.24
  167.7 2.7 copy-start.21
  167.7 2.7 copy-start.3
  167.7 2.7 copy-start.5
  167.8 14.6 %collective-permute-start = (f32[256,256]{1,0:T(8,128)S(1)}, f32[256,256]{1,0:T(8,128)S(1)}, u32[]{:S(2)}, u32[]{:S(2)}) collective-permute-start(f32[256,256]{1,0:T(8,128)S(1)} %divide_subtract_fusion.3), channel_id=1, source_target_pairs={{508,0},{0,4},{4,8},{8,12},{12,16},{16,20},{20,24},{24,28},{28,32}... | collective-permute-start | bytes 786440 | tf_op jit(solution)/shard_map/ppermute | solution.py:12
  224.8 3.6 copy-start.27
  270.4 3.6 copy-start.27
  274.1 2.2 copy-start
  276.3 319.9 %all-reduce.8.cloned.1.call-start = ((), (), s32[]{:S(2)}) async-start(), calls=%async_computation.1 | async-start | bytes 1048576 | tf_op jit(solution)/shard_map/psum | solution.py:102
  276.4 266.5 %copy-start.10 = (f32[2,256,256]{2,1,0:T(8,128)S(1)}, f32[2,256,256]{2,1,0:T(8,128)}, u32[]{:S(2)}) copy-start(f32[2,256,256]{2,1,0:T(8,128)} %param.20) | copy-start | bytes 1572868
  277.3 265.6 %copy-start.7 = (f32[2,256,256]{2,1,0:T(8,128)S(1)}, f32[2,256,256]{2,1,0:T(8,128)}, u32[]{:S(2)}) copy-start(f32[2,256,256]{2,1,0:T(8,128)} %param.19) | copy-start | bytes 1572868
  277.3 0.7 copy-start.25
  278.1 322.5 %collective-permute-start.1 = (f32[256]{0:T(256)S(1)}, f32[256]{0:T(256)S(1)}, u32[]{:S(2)}, u32[]{:S(2)}) collective-permute-start(f32[256]{0:T(256)S(1)} %copy-done.25), channel_id=1, source_target_pairs={{508,0},{0,4},{4,8},{8,12},{12,16},{16,20},{20,24},{24,28},{28,32}... | collective-permute-start | bytes 3080 | tf_op jit(solution)/shard_map/ppermute | solution.py:12
  542.9 55.0 %copy-start.6 = (f32[256,256]{1,0:T(8,128)S(1)}, f32[256,256]{1,0:T(8,128)}, u32[]{:S(2)}) copy-start(f32[256,256]{1,0:T(8,128)} %get-tuple-element.559) | copy-start | bytes 786436
  545.0 52.9 %copy-start.4 = (f32[256,256]{1,0:T(8,128)S(1)}, f32[256,256]{1,0:T(8,128)}, u32[]{:S(2)}) copy-start(f32[256,256]{1,0:T(8,128)} %param.17) | copy-start | bytes 786436
  596.2 1.1 copy-start.14
  596.2 1.1 copy-start.22
  598.6 1.8 copy-start.8
  (5 other events, 2.9 us)
Sparse Core Ops, SparseCore 0:
  106.5 58.7 all-reduce.9
  276.4 266.3 all-reduce.5
  546.7 49.4 all-reduce.7
where the time goes:
time: 609 us; the launch traced here: 608 us
  waiting for transfers between devices  383 us (63%)
  other arithmetic  158 us (26%)
  local copies, waits for them, and re-layouts  38.7 us (6%)
  between operations  14.1 us (2%)
  matrix products  9.56 us (2%)
    psum x1, waiting for transfers between devices, body(): operator_total = operator_total + lax.psum(operator_grad, ('blk', 'rep'))  263 us
    psum x2, waiting for transfers between devices, body(): left_sum, right_sum = lax.psum((left_grad, right_grad), 'rep')  108 us
    scatter-add x4, other arithmetic, step(): table_grad = table_grad.at[rel_row, src_row].add(query_grad)  104 us
    scatter-add x8, other arithmetic, step(): right_grad = right_grad.at[neg_row].add(neg_grad).at[dst_row].add(pos_grad)  28.1 us
    gather x4, local copies, waits for them, and re-layouts, batch_terms(): queries = query_table[rel_row, src_row]  12.7 us
  transfers between devices with their start and end apart: 5, of which 4 were waited for; matrix products, arithmetic and copies ran while one was open for 1% of the time, Pallas kernels for 0%

commit v1 on v0

--- a/solution.py
+++ b/solution.py
@@ -98,7 +98,7 @@
         left_grad, right_grad, operator_grad = bucket_terms(
             left_rows, right_rows, operator_bf, sources, targets, relations, negs, live_flags
         )
-        operator_total = operator_total + lax.psum(operator_grad, ("blk", "rep"))
+        operator_total = operator_total + lax.psum(lax.psum(operator_grad, "blk"), "rep")
         left_sum, right_sum = lax.psum((left_grad, right_grad), "rep")
         left_rows, left_accum = row_update(left_rows, left_accum, left_sum)
         right_rows, right_accum = row_update(right_rows, right_accum, right_sum)

time: 609 us -> 1440 us (2.36)
  waiting for transfers between devices: 383 us -> 1210 us
    psum x1, waiting for transfers between devices: 263 us -> 1030 us  [body(): lax.psum(operator_grad, 'blk')]
    psum x2, waiting for transfers between devices: 108 us -> 166 us  [body(): left_sum, right_sum = lax.psum((left_grad, right_grad), 'rep')]
where the time goes in v1:
time: 1440 us; the launch traced here: 1430 us
  waiting for transfers between devices  1210 us (84%)
  other arithmetic  158 us (11%)
  local copies, waits for them, and re-layouts  38 us (3%)
    psum x1, waiting for transfers between devices, body(): lax.psum(operator_grad, 'blk')  1030 us
    psum x2, waiting for transfers between devices, body(): left_sum, right_sum = lax.psum((left_grad, right_grad), 'rep')  166 us
    scatter-add x4, other arithmetic, step(): table_grad = table_grad.at[rel_row, src_row].add(query_grad)  104 us
  transfers between devices with their start and end apart: 5, of which 4 were waited for; matrix products, arithmetic and copies ran while one was open for 1% of the time, Pallas kernels for 0%

profile of v1, /device:TPU:1, one launch (start us, length us, event | category | flops | bytes accessed | tf_op | source)
XLA Modules:
  0.0 1434.1 jit_solution(17298234412777871406)
XLA Ops:
  14.1 91.3 %while.34 = (s32[]{:T(128)}, f32[2,256,256]{2,1,0:T(8,128)S(1)}, f32[256,256]{1,0:T(8,128)S(1)}, s32[2,512]{1,0:T(2,128)}, s32[2,512]{1,0:T(2,128)}, /*index=5*/...) while((s32[]{:T(128)}, f32[2,256,256]{2,1,0:T(8,128)S(1)}, ...), condition=%wide.region_7.8_spmd, body=%wide.region_0.7_spmd.sunk | while | flops 406075392 | bytes 12953801 | solution.py:62
  16.8 2.0 gather_fusion.1
  18.7 2.0 gather_fusion.2
  20.7 3.2 gather_fusion
  26.3 26.1 %scatter_fusion = f32[2,256,256]{2,1,0:T(8,128)S(1)} fusion(f32[2,256,256]{2,1,0:T(8,128)S(1)} %get-tuple-element.765, s32[512]{0:T(512)S(1)} %bitcast.154, f32[512,256]{1,0:T(8,128)S(1)} %convolution_add_fusion.5), kind=kCustom, calls=%fused_computation.6.clone.1 | custom fusion | flops 131072 | bytes 1576960 | tf_op jit(solution)/shard_map/while/body/eval_jaxpr/scatter-add | solution.py:57
  52.7 3.4 scatter_fusion.1
  56.1 3.6 scatter_custom_fusion.19
  62.4 2.0 gather_fusion.1
  64.4 2.0 gather_fusion.2
  66.3 3.2 gather_fusion
  71.9 26.1 %scatter_fusion = f32[2,256,256]{2,1,0:T(8,128)S(1)} fusion(f32[2,256,256]{2,1,0:T(8,128)S(1)} %get-tuple-element.765, s32[512]{0:T(512)S(1)} %bitcast.154, f32[512,256]{1,0:T(8,128)S(1)} %convolution_add_fusion.5), kind=kCustom, calls=%fused_computation.6.clone.1 | custom fusion | flops 131072 | bytes 1576960 | tf_op jit(solution)/shard_map/while/body/eval_jaxpr/scatter-add | solution.py:57
  98.3 3.4 scatter_fusion.1
  101.8 3.6 scatter_custom_fusion.19
  108.1 57.2 %all-reduce.10.cloned.1.call-done = (f32[256,256]{1,0:T(8,128)}, f32[256,256]{1,0:T(8,128)}) async-done(((f32[256,256]{1,0:T(8,128)}, f32[256,256]{1,0:T(8,128)}), (f32[256,256]{1,0:T(8,128)}, f32[256,256]{1,0:T(8,128)})) %all-reduce.10.cloned.1.call-update) | async-done | bytes 524304 | tf_op jit(solution)/shard_map/psum | solution.py:102
  167.8 2.5 collective-permute-start
  170.9 11.4 collective-permute-done
  182.7 91.3 %while.35 = (s32[]{:T(128)}, f32[2,256,256]{2,1,0:T(8,128)S(1)}, f32[256,256]{1,0:T(8,128)S(1)}, s32[2,512]{1,0:T(2,128)}, s32[2,512]{1,0:T(2,128)}, /*index=5*/...) while((s32[]{:T(128)}, f32[2,256,256]{2,1,0:T(8,128)S(1)}, ...), condition=%wide.region_19.20_spmd, body=%wide.region_12.19_spmd.sunk | while | flops 406075392 | bytes 12921097 | solution.py:62
  185.3 2.0 gather_fusion.4
  187.2 2.0 gather_fusion.5
  189.2 3.2 gather_fusion.3
  194.9 26.1 %scatter_fusion.2 = f32[2,256,256]{2,1,0:T(8,128)S(1)} fusion(f32[2,256,256]{2,1,0:T(8,128)S(1)} %get-tuple-element.798, s32[512]{0:T(512)S(1)} %bitcast.155, f32[512,256]{1,0:T(8,128)S(1)} %convolution_add_fusion.6), kind=kCustom, calls=%fused_computation.9.clone.1 | custom fusion | flops 131072 | bytes 1576960 | tf_op jit(solution)/shard_map/while/body/eval_jaxpr/scatter-add | solution.py:57
  221.3 3.4 scatter_fusion.3
  224.8 3.6 scatter_custom_fusion.23
  234.8 3.2 gather_fusion.3
  240.6 26.1 %scatter_fusion.2 = f32[2,256,256]{2,1,0:T(8,128)S(1)} fusion(f32[2,256,256]{2,1,0:T(8,128)S(1)} %get-tuple-element.798, s32[512]{0:T(512)S(1)} %bitcast.155, f32[512,256]{1,0:T(8,128)S(1)} %convolution_add_fusion.6), kind=kCustom, calls=%fused_computation.9.clone.1 | custom fusion | flops 131072 | bytes 1576960 | tf_op jit(solution)/shard_map/while/body/eval_jaxpr/scatter-add | solution.py:57
  267.0 3.4 scatter_fusion.3
  270.5 3.6 scatter_custom_fusion.23
  274.1 2.2 convolution_add_fusion.2
  277.3 1031.7 %all-reduce.6.cloned.1.call-done = f32[2,256,256]{2,1,0:T(8,128)} async-done(((f32[2,256,256]{2,1,0:T(8,128)}), f32[2,256,256]{2,1,0:T(8,128)}) %all-reduce.6.cloned.1.call-update) | async-done | bytes 524304 | tf_op jit(solution)/shard_map/psum | solution.py:101
  1309.1 2.1 collective-permute-start.1
  1311.1 108.5 %all-reduce.8.cloned.1.call-done = (f32[256,256]{1,0:T(8,128)}, f32[256,256]{1,0:T(8,128)}, f32[2,256,256]{2,1,0:T(8,128)}) async-done(((f32[256,256]{1,0:T(8,128)}, f32[256,256]{1,0:T(8,128)}, f32[2,256,256]{2,1,0:T(8,128)}), (f32[256,256]{1,0:T(8,128)}, f32[256,256]{1,0:T(8,128)}, f32[2,256,256]{2,1,0:T(8,128)})) %all-reduce.8.cloned.1.call-update) | async-done | bytes 1048592 | tf_op jit(solution)/shard_map/psum | solution.py:102
  1423.9 2.2 multiply_subtract_fusion
  (154 shorter events, 44.8 us)
Async XLA Ops:
  7.2 158.1 %all-reduce.10.cloned.1.call-start = ((), (), s32[]{:S(2)}) async-start(), calls=%async_computation.2 | async-start | bytes 1048576 | tf_op jit(solution)/shard_map/psum | solution.py:102
  10.6 1.1 copy-start.2
  12.0 0.7 copy-start.17
  12.0 0.7 copy-start.18
  12.7 0.7 copy-start.19
  12.7 0.7 copy-start.20
  14.1 1.2 copy-start.11
  56.1 3.6 copy-start.12
  59.7 1.2 copy-start.11
  101.8 3.6 copy-start.12
  105.4 0.9 copy-start.1
  106.3 1202.7 %all-reduce.6.cloned.1.call-start = ((), (), s32[]{:S(2)}) async-start(), calls=%async_computation | async-start | bytes 1048576 | tf_op jit(solution)/shard_map/psum | solution.py:101
  165.3 1.1 copy-start.9
  166.4 3.9 copy-start.13
  166.4 0.7 copy-start.24
  167.7 2.7 copy-start.21
  167.7 2.7 copy-start.3
  167.7 2.7 copy-start.5
  167.8 14.6 %collective-permute-start = (f32[256,256]{1,0:T(8,128)S(1)}, f32[256,256]{1,0:T(8,128)S(1)}, u32[]{:S(2)}, u32[]{:S(2)}) collective-permute-start(f32[256,256]{1,0:T(8,128)S(1)} %divide_subtract_fusion.3), channel_id=1, source_target_pairs={{508,0},{0,4},{4,8},{8,12},{12,16},{16,20},{20,24},{24,28},{28,32}... | collective-permute-start | bytes 786440 | tf_op jit(solution)/shard_map/ppermute | solution.py:12
  224.8 3.6 copy-start.27
  270.4 3.6 copy-start.27
  274.1 2.2 copy-start
  276.3 1143.4 %all-reduce.8.cloned.1.call-start = ((), (), s32[]{:S(2)}) async-start(), calls=%async_computation.1 | async-start | bytes 2097152 | tf_op jit(solution)/shard_map/psum | solution.py:102
  276.4 1032.7 %copy-start.25 = (f32[256]{0:T(256)S(1)}, f32[256]{0:T(256)}, u32[]{:S(2)}) copy-start(f32[256]{0:T(256)} %get-tuple-element.572) | copy-start | bytes 3076
  1309.0 112.3 %copy-start.6 = (f32[256,256]{1,0:T(8,128)S(1)}, f32[256,256]{1,0:T(8,128)}, u32[]{:S(2)}) copy-start(f32[256,256]{1,0:T(8,128)} %get-tuple-element.560) | copy-start | bytes 786436
  1309.0 112.3 %copy-start.4 = (f32[256,256]{1,0:T(8,128)S(1)}, f32[256,256]{1,0:T(8,128)}, u32[]{:S(2)}) copy-start(f32[256,256]{1,0:T(8,128)} %param.17) | copy-start | bytes 786436
  1309.1 117.1 %collective-permute-start.1 = (f32[256]{0:T(256)S(1)}, f32[256]{0:T(256)S(1)}, u32[]{:S(2)}, u32[]{:S(2)}) collective-permute-start(f32[256]{0:T(256)S(1)} %copy-done.25), channel_id=1, source_target_pairs={{508,0},{0,4},{4,8},{8,12},{12,16},{16,20},{20,24},{24,28},{28,32}... | collective-permute-start | bytes 3080 | tf_op jit(solution)/shard_map/ppermute | solution.py:12
  1419.7 1.1 copy-start.14
  1419.7 1.1 copy-start.22
  1422.0 1.9 copy-start.7
  1422.0 1.9 copy-start.10
  1423.9 2.2 copy-start.8
  (5 other events, 2.9 us)
Sparse Core Ops, SparseCore 0:
  106.5 58.7 all-reduce.9
  276.4 1032.5 all-reduce.5
  1313.1 106.5 all-reduce.7
